TPU v7x, 32 devices: a whole 2x2x4 slice. The times are simulated.
32 devices in a mesh: groups: 1, seq: 32 (over z, y, x, core).
Axes of the slice: x: 2, y: 2, z: 4, core: 2. Of those that a mesh axis runs over, the one named last changes fastest.
Arguments:
- features: bfloat16 [2, 4096, 1536], P('groups', 'seq'), may hold values from -6 to 6
- cotangent: bfloat16 [2, 4096, 1536], P('groups', 'seq'), may hold values from -6 to 6
- dilated_kernel_weight: bfloat16 [1536, 3, 768], P('seq'), may hold values from -0.09375 to 0.09375
- project_weight: bfloat16 [1536, 768], P('seq'), may hold values from -0.21875 to 0.21875
- outer_gain: float32 [1536], replicated, may hold values from 0.1 to 1.9
- inner_gain: float32 [768], replicated, may hold values from 0.1 to 1.9
Outputs:
- block_out: bfloat16 [2, 4096, 1536], P('groups', 'seq')
- grad_features: bfloat16 [2, 4096, 1536], P('groups', 'seq')
- grad_dilated: float32 [1536, 3, 768], P(('groups', 'seq'))
- grad_project: float32 [1536, 768], P(('groups', 'seq'))
- grad_outer_gain: float32 [1536], P(('groups', 'seq'))
- grad_inner_gain: float32 [768], P(('groups', 'seq'))
All inputs are finite; a program needn't handle non-finite values.
Results may differ from a plain program's by a relative error of at most 0.0056.
Values may be sent and summed in bfloat16 or wider, within the bound.
No kernel may reach another device: no remote copies, remote signals or barrier semaphores. Data moves between devices by JAX's collectives and lax.ppermute only.
A program may use at most 128 MiB of HBM per device.

v0:
```python
import math
import jax
import jax.numpy as jnp
from jax import lax
from jax.sharding import PartitionSpec as P

KERNEL_TAPS = 3
DILATION_STEP = 32
eps = 1e-06


def padded(block, sides, width):
    for axis, dim in sides:
        count = lax.axis_size(axis)
        forward = [(i, i + 1) for i in range(count - 1)]
        backward = [(target, source) for source, target in forward]
        low = lax.ppermute(
            lax.slice_in_dim(block, block.shape[dim] - width, None, axis=dim), axis, forward
        )
        high = lax.ppermute(lax.slice_in_dim(block, 0, width, axis=dim), axis, backward)
        block = jnp.concatenate([low, block, high], axis=dim)
    return block


def act_norm(values, gain):
    meansq = jnp.mean(values * values, axis=-1, keepdims=True)
    return jax.nn.gelu(values * lax.rsqrt(meansq + eps) * gain, approximate=True)


def reduce_dilated(padded_input, conv_output_gradient, factor):
    bin_count = conv_output_gradient.shape[1]
    tap_slices = [
        jnp.einsum(
            "btc,bti->ci",
            padded_input[:, tap_index * DILATION_STEP : tap_index * DILATION_STEP + bin_count],
            conv_output_gradient,
            preferred_element_type=jnp.float32,
        )
        for tap_index in range(KERNEL_TAPS)
    ]
    return lax.psum_scatter(
        jnp.stack(tap_slices, axis=1) * factor, "seq", scatter_dimension=0, tiled=True
    )


def body(features, cotangent, dilated_kernel_weight, project_weight, outer_gain, inner_gain):
    bin_count = features.shape[1]
    factor = 1.0 / math.sqrt(features.shape[0] * bin_count * lax.axis_size("seq"))
    full_dilated = lax.all_gather(dilated_kernel_weight, "seq", axis=0, tiled=True)
    full_project = lax.all_gather(project_weight, "seq", axis=0, tiled=True)
    as_float = features.astype(jnp.float32)
    active_features = act_norm(as_float, outer_gain).astype(jnp.bfloat16)
    padded_input = padded(active_features, (("seq", 1),), DILATION_STEP)
    conv_output = jnp.einsum(
        "btc,ci->bti",
        padded_input[:, 0:bin_count],
        full_dilated[:, 0, :],
        preferred_element_type=jnp.float32,
    )
    for tap_index in range(1, KERNEL_TAPS):
        conv_output = conv_output + jnp.einsum(
            "btc,ci->bti",
            padded_input[:, tap_index * DILATION_STEP : tap_index * DILATION_STEP + bin_count],
            full_dilated[:, tap_index, :],
            preferred_element_type=jnp.float32,
        )
    hidden = act_norm(conv_output, inner_gain).astype(jnp.bfloat16)
    block_out = (
        as_float
        + jnp.einsum("bti,ci->btc", hidden, full_project, preferred_element_type=jnp.float32)
    ).astype(jnp.bfloat16)
    grad_hidden = jnp.einsum(
        "btc,ci->bti", cotangent, full_project, preferred_element_type=jnp.float32
    )
    unused, pull_inner = jax.vjp(act_norm, conv_output, inner_gain)
    conv_output_gradient, grad_gain_inner = pull_inner(grad_hidden)
    conv_output_gradient = conv_output_gradient.astype(jnp.bfloat16)
    padded_input_gradient = padded(conv_output_gradient, (("seq", 1),), DILATION_STEP)
    grad_active = jnp.zeros(features.shape, jnp.float32)
    for tap_index in range(KERNEL_TAPS):
        tap_shift = (KERNEL_TAPS - 1 - tap_index) * DILATION_STEP
        grad_active = grad_active + jnp.einsum(
            "bti,ci->btc",
            padded_input_gradient[:, tap_shift : tap_shift + bin_count],
            full_dilated[:, tap_index, :],
            preferred_element_type=jnp.float32,
        )
    unused_two, pull_outer = jax.vjp(act_norm, as_float, outer_gain)
    grad_branch, grad_gain_outer = pull_outer(grad_active)
    grad_features = (cotangent.astype(jnp.float32) + grad_branch).astype(jnp.bfloat16)
    grad_dilated = reduce_dilated(padded_input, conv_output_gradient, factor)
    grad_project = lax.psum_scatter(
        jnp.einsum("btc,bti->ci", cotangent, hidden, preferred_element_type=jnp.float32) * factor,
        "seq",
        scatter_dimension=0,
        tiled=True,
    )
    grad_outer_gain, grad_inner_gain = (
        lax.psum_scatter(grad_gain_outer * factor, "seq", scatter_dimension=0, tiled=True),
        lax.psum_scatter(grad_gain_inner * factor, "seq", scatter_dimension=0, tiled=True),
    )
    return (block_out, grad_features, grad_dilated, grad_project, grad_outer_gain, grad_inner_gain)


def solution(mesh):
    return jax.shard_map(
        body,
        mesh=mesh,
        in_specs=(
            P("groups", "seq", None),
            P("groups", "seq", None),
            P("seq", None, None),
            P("seq", None),
            P(),
            P(),
        ),
        out_specs=(
            P("groups", "seq", None),
            P("groups", "seq", None),
            P(("groups", "seq"), None, None),
            P(("groups", "seq"), None),
            P(("groups", "seq")),
            P(("groups", "seq")),
        ),
        check_vma=False,
    )
```

profile of v0, /device:TPU:0, one launch (start us, length us, event | category | flops | bytes accessed | tf_op | source)
XLA Modules:
  0.0 433.5 jit_solution(2068119754786179202)
XLA Ops:
  7.2 0.0 copy-start
  7.2 0.0 all-gather.3.cloned.1.call-start
  7.2 0.7 all-gather.3.cloned.1.call-update
  7.9 0.0 all-gather.5.cloned.1.call-start
  8.0 0.7 all-gather.5.cloned.1.call-update
  8.7 0.0 reduce-scatter.7.cloned.1.call-start
  8.7 1.4 fusion.27
  10.1 0.0 copy-done
  10.1 0.0 copy-start.8
  10.1 1.4 fusion.18
  11.5 2.4 collective-permute-start
  13.9 1.3 collective-permute-start.1
  15.2 71.3 %all-gather.3.cloned.1.call-done = bf16[1536,3,768]{2,0,1:T(8,128)(2,1)} async-done(((bf16[48,3,768]{2,0,1:T(8,128)(2,1)}), bf16[1536,3,768]{2,0,1:T(8,128)(2,1)}) %all-gather.3.cloned.1.call-update) | async-done | bytes 7077904 | tf_op jit(solution)/shard_map/all_gather | solution.py:49
  86.5 2.4 fusion.8
  89.0 0.0 copy-done.8
  89.0 0.0 collective-permute-done.1
  89.0 0.0 copy-start.4
  89.0 2.5 fusion.10
  91.5 0.0 copy-done.4
  91.5 0.0 copy-start.1
  91.5 0.0 copy-start.6
  91.5 0.0 collective-permute-done
  91.5 0.0 copy-start.2
  91.6 2.6 multiply_reduce_fusion.2
  94.2 0.0 copy-done.2
  94.2 0.0 copy-done.1
  94.2 0.0 copy-done.6
  94.2 3.2 fusion
  97.4 6.1 %copy.26 = f32[1536,768]{1,0:T(8,128)} copy(f32[1536,768]{0,1:T(8,128)} %fusion) | data formatting | bytes 9437184
  103.5 0.0 reduce-scatter.7.cloned.1.call-update
  103.5 0.0 reduce-scatter.5.cloned.1.call-start
  103.6 41.6 %all-gather.5.cloned.1.call-done = bf16[1536,768]{1,0:T(8,128)(2,1)} async-done(((bf16[48,768]{1,0:T(8,128)(2,1)}), bf16[1536,768]{1,0:T(8,128)(2,1)}) %all-gather.5.cloned.1.call-update) | async-done | bytes 2359312 | tf_op jit(solution)/shard_map/all_gather | solution.py:50
  145.2 3.6 multiply_reduce_fusion
  148.9 0.2 fusion.37
  149.1 0.7 copy-done.3
  149.8 0.0 copy-start.5
  149.8 0.8 convolution_bitcast_fusion.2
  150.6 0.1 copy-done.5
  150.7 0.8 convolution_bitcast_fusion
  151.5 0.8 convolution_bitcast_fusion.1
  152.4 5.5 %maximum_multiply_fusion = f32[1536,3,768]{2,0,1:T(8,128)} fusion(f32[1536,1,768]{2,0,1:T(8,128)S(1)} %convolution_bitcast_fusion, f32[1536,1,768]{2,0,1:T(8,128)S(1)} %convolution_bitcast_fusion.1, f32[1536,1,768]{2,0,1:T(8,128)S(1)} %convolution_bitcast_fusion.2), kind=kLoop, calls=%fused_computation | loop fusion | flops 10616832 | bytes 28311552 | tf_op jit(solution)/shard_map/mul | solution.py:42
  157.8 0.0 reduce-scatter.5.cloned.1.call-update
  157.9 0.0 copy-start.11
  157.9 2.3 collective-permute-start.3
  160.2 2.5 fusion.7
  162.8 0.0 copy-done.11
  162.8 0.0 copy-start.10
  162.8 1.9 fusion.2
  164.6 0.0 copy-done.10
  164.6 0.0 copy-start.7
  164.6 1.6 collective-permute-start.2
  166.3 0.0 collective-permute-done.3
  166.3 2.5 fusion.9
  168.8 0.0 collective-permute-done.2
  168.8 0.0 copy-done.7
  168.8 0.0 copy-done.9
  168.9 4.4 %fusion.21 = (f32[1536]{0:T(1024)S(1)}, f32[2,128]{1,0:T(2,128)}, f32[2,128,1536]{2,1,0:T(8,128)S(1)}) fusion(bf16[2,128,1536]{2,1,0:T(8,128)(2,1)S(1)} %copy-done, f32[2,128]{1,0:T(2,128)S(1)} %copy-done.9, f32[1536]{0:T(1024)S(1)} %copy-done.7, f32[2,128,1536]{2,1,0:T(8,128)S(1)} %fusion.9, f32[2,128,1536]{2,1,0:T(8,128)S(1)} %fusion.7, ...), kind=kOutput, calls=%fused_computation.38 | convolution fusion | flops 616167680 | bytes 8370176 | tf_op jit(solution)/shard_map/bti,ci->btc/dot_general | solution.py:82
  173.3 42.5 %all-reduce.2 = (f32[1536]{0:T(1024)S(1)}, f32[768]{0:T(1024)S(1)}) all-reduce(f32[1536]{0:T(1024)S(1)} %broadcast_multiply_fusion, f32[768]{0:T(1024)S(1)} %broadcast_multiply_fusion.1), channel_id=4, replica_groups=mesh['groups'=1,'seq'=32] {'seq'}, use_global_device_ids=true, to_apply=%region_7.0.clone | all-reduce | flops 2304 | bytes 18432
  215.8 0.6 dynamic-slice
  216.4 0.6 dynamic-slice.1
  217.0 0.7 multiply_multiply_fusion.5
  217.7 2.1 fusion.26
  219.8 37.8 %reduce-scatter.7.cloned.1.call-done = f32[48,768]{1,0:T(8,128)} async-done(((f32[1536,768]{1,0:T(8,128)}), f32[48,768]{1,0:T(8,128)}) %reduce-scatter.7.cloned.1.call-update) | async-done | bytes 147472
  257.5 169.5 %reduce-scatter.5.cloned.1.call-done = f32[48,3,768]{2,0,1:T(8,128)} async-done(((f32[1536,3,768]{2,0,1:T(8,128)}), f32[48,3,768]{2,0,1:T(8,128)}) %reduce-scatter.5.cloned.1.call-update) | async-done | bytes 442384 | tf_op jit(solution)/shard_map/reduce_scatter | solution.py:41
  (9 shorter events, 0.1 us)
Async XLA Ops:
  7.2 2.9 copy-start
  7.2 79.3 %all-gather.3.cloned.1.call-start = ((), (), s32[]{:S(2)}) async-start(), calls=%async_computation.2 | async-start | bytes 7299072 | tf_op jit(solution)/shard_map/all_gather | solution.py:49
  7.9 137.3 %all-gather.5.cloned.1.call-start = ((), (), s32[]{:S(2)}) async-start(), calls=%async_computation.3 | async-start | bytes 2433024 | tf_op jit(solution)/shard_map/all_gather | solution.py:50
  8.7 248.9 %reduce-scatter.7.cloned.1.call-start = ((), (), s32[]{:S(2)}) async-start(), calls=%async_computation.5 | async-start | bytes 4866048
  10.1 78.9 %copy-start.8 = (f32[2,128]{1,0:T(2,128)}, f32[2,128]{1,0:T(2,128)S(1)}, u32[]{:S(2)}) copy-start(f32[2,128]{1,0:T(2,128)S(1)} %fusion.42) | copy-start | bytes 3076
  11.5 80.0 %collective-permute-start = (bf16[2,32,1536]{2,1,0:T(8,128)(2,1)S(1)}, bf16[2,32,1536]{2,1,0:T(8,128)(2,1)S(1)}, u32[]{:S(2)}, u32[]{:S(2)}) collective-permute-start(bf16[2,32,1536]{2,1,0:T(8,128)(2,1)S(1)} %get-tuple-element.24), channel_id=1, source_target_pairs={{0,1},{1,2},{2,3},{3,4},{4,5},{5,6},{6,7},{7,8},{8,9},{9,10},{10,1... | collective-permute-start | bytes 589832 | tf_op jit(solution)/shard_map/ppermute | solution.py:17
  13.9 75.0 %collective-permute-start.1 = (bf16[2,32,1536]{2,1,0:T(8,128)(2,1)S(1)}, bf16[2,32,1536]{2,1,0:T(8,128)(2,1)S(1)}, u32[]{:S(2)}, u32[]{:S(2)}) collective-permute-start(bf16[2,32,1536]{2,1,0:T(8,128)(2,1)S(1)} %get-tuple-element.25), channel_id=1, source_target_pairs={{1,0},{2,1},{3,2},{4,3},{5,4},{6,5},{7,6},{8,7},{9,8},{10,9},{11,1... | collective-permute-start | bytes 589832 | tf_op jit(solution)/shard_map/ppermute | solution.py:20
  89.0 2.5 copy-start.4
  91.5 2.7 copy-start.1
  91.5 2.7 copy-start.6
  91.5 2.7 copy-start.2
  103.5 323.5 %reduce-scatter.5.cloned.1.call-start = ((), (), s32[]{:S(2)}) async-start(), calls=%async_computation.4 | async-start | bytes 14598144 | tf_op jit(solution)/shard_map/reduce_scatter | solution.py:41
  148.8 0.9 copy-start.3
  149.8 0.9 copy-start.5
  157.9 4.9 %copy-start.11 = (bf16[1536,768]{1,0:T(8,128)(2,1)S(1)}, bf16[1536,768]{1,0:T(8,128)(2,1)}, u32[]{:S(2)}) copy-start(bf16[1536,768]{1,0:T(8,128)(2,1)} %all-gather.5.cloned.1.call-done) | copy-start | bytes 7077892
  157.9 8.4 %collective-permute-start.3 = (bf16[2,32,768]{2,1,0:T(8,128)(2,1)S(1)}, bf16[2,32,768]{2,1,0:T(8,128)(2,1)S(1)}, u32[]{:S(2)}, u32[]{:S(2)}) collective-permute-start(bf16[2,32,768]{2,1,0:T(8,128)(2,1)S(1)} %get-tuple-element.27), channel_id=1, source_target_pairs={{0,1},{1,2},{2,3},{3,4},{4,5},{5,6},{6,7},{7,8},{8,9},{9,10},{10,1... | collective-permute-start | bytes 294920 | tf_op jit(solution)/shard_map/ppermute | solution.py:17
  162.8 1.9 copy-start.10
  164.6 4.2 copy-start.7
  164.6 4.2 copy-start.9
  164.6 4.2 collective-permute-start.2
Sparse Core Ops, SparseCore 0:
  11.0 75.5 all-gather.2
  89.4 55.7 all-gather.4
  151.3 106.2 reduce-scatter.6
  265.0 161.9 reduce-scatter.4
where the time goes:
time: 434 us
  waiting for transfers between devices  322 us (74%)
  blocking collectives  42.5 us (10%)
  matrix products  28.2 us (6%)
  between operations  14.1 us (3%)
  other arithmetic  11.2 us (3%)
  local copies, waits for them, and re-layouts  8.18 us (2%)
  starting transfers between devices  7.73 us (2%)
    reduce_scatter x1, waiting for transfers between devices, reduce_dilated(): lax.psum_scatter(jnp.stack(tap_slices, axis=1) * factor, 'seq', scatter_d...  169 us
    all_gather x1, waiting for transfers between devices, body(): lax.all_gather(dilated_kernel_weight, 'seq', axis=0, tiled=True)  71.3 us
    unnamed x1, blocking collectives  42.5 us
    all_gather x1, waiting for transfers between devices, body(): full_project = lax.all_gather(project_weight, 'seq', axis=0, tiled=True)  41.6 us
    unnamed x5, waiting for transfers between devices  39.2 us
    dot_general x3, matrix products, body(): jnp.einsum('bti,ci->btc', padded_input_gradient[:, tap_shift:tap_shift +...  9.53 us
  transfers between devices with their start and end apart: 8, of which 4 were waited for; matrix products, arithmetic and copies ran while one was open for 11% of the time, Pallas kernels for 0%

commit v1 on v0

--- a/solution.py
+++ b/solution.py
@@ -47,7 +47,15 @@
     bin_count = features.shape[1]
     factor = 1.0 / math.sqrt(features.shape[0] * bin_count * lax.axis_size("seq"))
     full_dilated = lax.all_gather(dilated_kernel_weight, "seq", axis=0, tiled=True)
-    full_project = lax.all_gather(project_weight, "seq", axis=0, tiled=True)
+    u1, odd, upper = (lax.axis_size("seq"), lax.axis_index("seq"), project_weight.shape[0])
+    left_arr, f_next = (project_weight, 1)
+    while f_next < u1:
+        left_arr = jnp.concatenate(
+            [left_arr, lax.ppermute(left_arr, "seq", [(c, (c - f_next) % u1) for c in range(u1)])],
+            axis=0,
+        )
+        f_next = 2 * f_next
+    full_project = jnp.roll(left_arr, odd * upper, axis=0)
     as_float = features.astype(jnp.float32)
     active_features = act_norm(as_float, outer_gain).astype(jnp.bfloat16)
     padded_input = padded(active_features, (("seq", 1),), DILATION_STEP)

time: 434 us -> 403 us (0.929)
  waiting for transfers between devices: 322 us -> 264 us
  starting transfers between devices: 7.73 us -> 20.6 us
  local copies, waits for them, and re-layouts: 8.18 us -> 18.9 us
    ppermute x0 -> x5, waiting for transfers between devices: none -> 87.2 us  [body(): lax.ppermute(left_arr, 'seq', [(c, (c - f_next) % u1) for c in range(u1)])]
    reduce_scatter x1, waiting for transfers between devices: 169 us -> 106 us  [reduce_dilated(): lax.psum_scatter(jnp.stack(tap_slices, axis=1) * factor, 'seq', scatter_d...]
    all_gather x1 -> x0, waiting for transfers between devices: 41.6 us -> none  [body(): full_project = lax.all_gather(project_weight, 'seq', axis=0, tiled=True)]
    unnamed x5 -> x4, waiting for transfers between devices: 39.2 us -> 0.72 us
    ppermute x0 -> x5, starting transfers between devices: none -> 15 us  [body(): lax.ppermute(left_arr, 'seq', [(c, (c - f_next) % u1) for c in range(u1)])]
    unnamed x27 -> x43, local copies, waits for them, and re-layouts: 8.13 us -> 16.6 us
    all_gather x1, waiting for transfers between devices: 71.3 us -> 66.3 us  [body(): lax.all_gather(dilated_kernel_weight, 'seq', axis=0, tiled=True)]
    ppermute x2, waiting for transfers between devices: 0.01 us -> 4.46 us  [padded(): lax.ppermute(lax.slice_in_dim(block, 0, width, axis=dim), axis, backward)]
  transfers between devices with their start and end apart: 8 -> 12, of which waited for: 4 -> 7; matrix products, arithmetic and copies ran while one was open for 11% -> 15% of each run, Pallas kernels for 0% -> 0%
where the time goes in v1:
time: 403 us; the launch traced here: 402 us
  waiting for transfers between devices  264 us (66%)
  blocking collectives  42.8 us (11%)
  matrix products  29.6 us (7%)
  starting transfers between devices  20.6 us (5%)
  local copies, waits for them, and re-layouts  18.9 us (5%)
  between operations  14.1 us (3%)
  other arithmetic  11.7 us (3%)
    reduce_scatter x1, waiting for transfers between devices, reduce_dilated(): lax.psum_scatter(jnp.stack(tap_slices, axis=1) * factor, 'seq', scatter_d...  106 us
    ppermute x5, waiting for transfers between devices, body(): lax.ppermute(left_arr, 'seq', [(c, (c - f_next) % u1) for c in range(u1)])  87.2 us
    all_gather x1, waiting for transfers between devices, body(): lax.all_gather(dilated_kernel_weight, 'seq', axis=0, tiled=True)  66.3 us
    unnamed x1, blocking collectives  42.8 us
    unnamed x43, local copies, waits for them, and re-layouts  16.6 us
    ppermute x5, starting transfers between devices, body(): lax.ppermute(left_arr, 'seq', [(c, (c - f_next) % u1) for c in range(u1)])  15 us
    dot_general x3, matrix products, body(): jnp.einsum('bti,ci->btc', padded_input_gradient[:, tap_shift:tap_shift +...  9.47 us
  transfers between devices with their start and end apart: 12, of which 7 were waited for; matrix products, arithmetic and copies ran while one was open for 15% of the time, Pallas kernels for 0%

profile of v1, /device:TPU:0, one launch (start us, length us, event | category | flops | bytes accessed | tf_op | source)
XLA Modules:
  0.0 401.9 jit_solution(3701750761538321572)
XLA Ops:
  7.2 0.0 all-gather.2.cloned.1.call-start
  7.2 0.7 all-gather.2.cloned.1.call-update
  7.9 0.0 reduce-scatter.7.cloned.1.call-start
  7.9 6.4 %collective-permute-start.2 = (bf16[48,768]{1,0:T(8,128)(2,1)}, bf16[48,768]{1,0:T(8,128)(2,1)S(1)}, u32[]{:S(2)}, u32[]{:S(2)}) collective-permute-start(bf16[48,768]{1,0:T(8,128)(2,1)} %param.9), channel_id=1, source_target_pairs={{0,31},{1,0},{2,1},{3,2},{4,3},{5,4},{6,5},{7,6},{8,7},{9,8},{10,9... | collective-permute-start | bytes 221192 | tf_op jit(solution)/shard_map/ppermute | solution.py:54
  14.4 1.4 fusion.29
  15.8 1.8 fusion.20
  17.6 1.3 collective-permute-start
  19.0 1.3 collective-permute-start.1
  20.3 66.3 %all-gather.2.cloned.1.call-done = bf16[1536,3,768]{2,0,1:T(8,128)(2,1)} async-done(((bf16[48,3,768]{2,0,1:T(8,128)(2,1)}), bf16[1536,3,768]{2,0,1:T(8,128)(2,1)}) %all-gather.2.cloned.1.call-update) | async-done | bytes 7077904 | tf_op jit(solution)/shard_map/all_gather | solution.py:49
  86.5 2.4 fusion.8
  89.0 0.0 copy-start.9
  89.0 2.5 fusion.10
  91.5 0.0 copy-start.1
  91.5 0.0 copy-start.11
  91.6 2.6 multiply_reduce_fusion.2
  94.2 3.1 fusion
  97.4 6.1 %copy.26 = f32[1536,768]{1,0:T(8,128)} copy(f32[1536,768]{0,1:T(8,128)} %fusion) | data formatting | bytes 9437184
  103.5 0.0 reduce-scatter.7.cloned.1.call-update
  103.5 0.0 reduce-scatter.5.cloned.1.call-start
  103.6 0.8 copy-done.6
  104.4 2.8 collective-permute-start.3
  107.2 3.5 collective-permute-done.3
  110.8 2.5 collective-permute-start.4
  113.3 5.9 %collective-permute-done.4 = bf16[192,768]{1,0:T(8,128)(2,1)S(1)} collective-permute-done((bf16[192,768]{1,0:T(8,128)(2,1)S(1)}, bf16[192,768]{1,0:T(8,128)(2,1)S(1)}, u32[]{:S(2)}, u32[]{:S(2)}) %collective-permute-start.4) | collective-permute-done | bytes 294944 | tf_op jit(solution)/shard_map/ppermute | solution.py:54
  119.2 1.6 collective-permute-start.5
  120.9 0.7 constant_dynamic-update-slice_fusion.4
  121.5 0.7 constant_dynamic-update-slice_fusion.3
  122.2 0.7 constant_dynamic-update-slice_fusion.2
  122.9 0.9 constant_dynamic-update-slice_fusion.1
  123.8 9.2 %collective-permute-done.5 = bf16[384,768]{1,0:T(8,128)(2,1)S(1)} collective-permute-done((bf16[384,768]{1,0:T(8,128)(2,1)S(1)}, bf16[384,768]{1,0:T(8,128)(2,1)S(1)}, u32[]{:S(2)}, u32[]{:S(2)}) %collective-permute-start.5) | collective-permute-done | bytes 589856 | tf_op jit(solution)/shard_map/ppermute | solution.py:54
  133.0 1.2 constant_dynamic-update-slice_fusion
  134.2 0.0 copy-done.4
  134.2 1.6 collective-permute-start.6
  135.8 68.5 %collective-permute-done.6 = bf16[768,768]{1,0:T(8,128)(2,1)S(1)} collective-permute-done((bf16[768,768]{1,0:T(8,128)(2,1)}, bf16[768,768]{1,0:T(8,128)(2,1)S(1)}, u32[]{:S(2)}, u32[]{:S(2)}) %collective-permute-start.6) | collective-permute-done | bytes 1179680 | tf_op jit(solution)/shard_map/ppermute | solution.py:54
  204.3 1.1 constant_dynamic-update-slice_fusion.11
  205.4 0.6 constant_dynamic-update-slice_fusion.10
  206.1 0.6 constant_dynamic-update-slice_fusion.9
  206.7 0.7 constant_dynamic-update-slice_fusion.8
  207.4 0.7 constant_dynamic-update-slice_fusion.7
  208.1 0.9 constant_dynamic-update-slice_fusion.6
  209.0 1.1 constant_dynamic-update-slice_fusion.5
  210.1 3.1 multiply_reduce_fusion
  213.3 0.2 fusion.42
  213.5 0.7 copy-done.8
  214.2 0.8 convolution_bitcast_fusion.2
  215.0 0.1 copy-done.10
  215.1 0.8 convolution_bitcast_fusion
  215.9 0.8 convolution_bitcast_fusion.1
  216.8 5.4 %maximum_multiply_fusion = f32[1536,3,768]{2,0,1:T(8,128)} fusion(f32[1536,1,768]{2,0,1:T(8,128)S(1)} %convolution_bitcast_fusion, f32[1536,1,768]{2,0,1:T(8,128)S(1)} %convolution_bitcast_fusion.1, f32[1536,1,768]{2,0,1:T(8,128)S(1)} %convolution_bitcast_fusion.2), kind=kLoop, calls=%fused_computation | loop fusion | flops 10616832 | bytes 28311552 | tf_op jit(solution)/shard_map/mul | solution.py:42
  222.2 0.0 reduce-scatter.5.cloned.1.call-update
  222.3 1.4 collective-permute-start.8
  223.7 3.8 fusion.2
  227.5 2.5 fusion.7
  230.0 0.0 copy-start.12
  230.0 1.5 collective-permute-start.7
  231.5 2.5 fusion.9
  234.0 4.5 %collective-permute-done.7 = bf16[2,32,768]{2,1,0:T(8,128)(2,1)S(1)} collective-permute-done((bf16[2,32,768]{2,1,0:T(8,128)(2,1)S(1)}, bf16[2,32,768]{2,1,0:T(8,128)(2,1)S(1)}, u32[]{:S(2)}, u32[]{:S(2)}) %collective-permute-start.7) | collective-permute-done | bytes 98336 | tf_op jit(solution)/shard_map/ppermute | solution.py:20
  238.5 4.5 %fusion.23 = (f32[1536]{0:T(1024)S(1)}, f32[2,128]{1,0:T(2,128)}, f32[2,128,1536]{2,1,0:T(8,128)S(1)}) fusion(bf16[2,128,1536]{2,1,0:T(8,128)(2,1)S(1)} %copy-done, f32[2,128]{1,0:T(2,128)S(1)} %copy-done.14, f32[1536]{0:T(1024)S(1)} %copy-done.12, f32[2,128,1536]{2,1,0:T(8,128)S(1)} %fusion.9, f32[2,128,1536]{2,1,0:T(8,128)S(1)} %fusion.7, ...), kind=kOutput, calls=%fused_computation.40 | convolution fusion | flops 616167680 | bytes 8370176 | tf_op jit(solution)/shard_map/bti,ci->btc/dot_general | solution.py:90
  243.0 42.8 %all-reduce.2 = (f32[1536]{0:T(1024)S(1)}, f32[768]{0:T(1024)S(1)}) all-reduce(f32[1536]{0:T(1024)S(1)} %broadcast_multiply_fusion, f32[768]{0:T(1024)S(1)} %broadcast_multiply_fusion.1), channel_id=4, replica_groups=mesh['groups'=1,'seq'=32] {'seq'}, use_global_device_ids=true, to_apply=%region_7.8.clone | all-reduce | flops 2304 | bytes 18432
  285.8 0.6 dynamic-slice
  286.4 0.6 dynamic-slice.1
  287.0 0.7 multiply_multiply_fusion.5
  287.7 2.1 fusion.28
  289.7 105.7 %reduce-scatter.5.cloned.1.call-done = f32[48,3,768]{2,0,1:T(8,128)} async-done(((f32[1536,3,768]{2,0,1:T(8,128)}), f32[48,3,768]{2,0,1:T(8,128)}) %reduce-scatter.5.cloned.1.call-update) | async-done | bytes 442384 | tf_op jit(solution)/shard_map/reduce_scatter | solution.py:41
  (37 shorter events, 0.2 us)
Async XLA Ops:
  7.2 79.3 %all-gather.2.cloned.1.call-start = ((), (), s32[]{:S(2)}) async-start(), calls=%async_computation.2 | async-start | bytes 7299072 | tf_op jit(solution)/shard_map/all_gather | solution.py:49
  7.9 281.8 %reduce-scatter.7.cloned.1.call-start = ((), (), s32[]{:S(2)}) async-start(), calls=%async_computation.4 | async-start | bytes 4866048
  7.9 95.6 %collective-permute-start.2 = (bf16[48,768]{1,0:T(8,128)(2,1)}, bf16[48,768]{1,0:T(8,128)(2,1)S(1)}, u32[]{:S(2)}, u32[]{:S(2)}) collective-permute-start(bf16[48,768]{1,0:T(8,128)(2,1)} %param.9), channel_id=1, source_target_pairs={{0,31},{1,0},{2,1},{3,2},{4,3},{5,4},{6,5},{7,6},{8,7},{9,8},{10,9... | collective-permute-start | bytes 221192 | tf_op jit(solution)/shard_map/ppermute | solution.py:54
  15.7 73.2 %copy-start.13 = (f32[2,128]{1,0:T(2,128)}, f32[2,128]{1,0:T(2,128)S(1)}, u32[]{:S(2)}) copy-start(f32[2,128]{1,0:T(2,128)S(1)} %fusion.47) | copy-start | bytes 3076
  17.6 73.9 %collective-permute-start = (bf16[2,32,1536]{2,1,0:T(8,128)(2,1)S(1)}, bf16[2,32,1536]{2,1,0:T(8,128)(2,1)S(1)}, u32[]{:S(2)}, u32[]{:S(2)}) collective-permute-start(bf16[2,32,1536]{2,1,0:T(8,128)(2,1)S(1)} %get-tuple-element.24), channel_id=1, source_target_pairs={{0,1},{1,2},{2,3},{3,4},{4,5},{5,6},{6,7},{7,8},{8,9},{9,10},{10,1... | collective-permute-start | bytes 589832 | tf_op jit(solution)/shard_map/ppermute | solution.py:17
  19.0 70.0 %collective-permute-start.1 = (bf16[2,32,1536]{2,1,0:T(8,128)(2,1)S(1)}, bf16[2,32,1536]{2,1,0:T(8,128)(2,1)S(1)}, u32[]{:S(2)}, u32[]{:S(2)}) collective-permute-start(bf16[2,32,1536]{2,1,0:T(8,128)(2,1)S(1)} %get-tuple-element.25), channel_id=1, source_target_pairs={{1,0},{2,1},{3,2},{4,3},{5,4},{6,5},{7,6},{8,7},{9,8},{10,9},{11,1... | collective-permute-start | bytes 589832 | tf_op jit(solution)/shard_map/ppermute | solution.py:20
  89.0 2.5 copy-start.9
  91.5 2.7 copy-start.1
  91.5 2.7 copy-start.11
  91.5 2.7 copy-start.7
  103.5 0.9 copy-start.6
  103.5 291.8 %reduce-scatter.5.cloned.1.call-start = ((), (), s32[]{:S(2)}) async-start(), calls=%async_computation.3 | async-start | bytes 14598144 | tf_op jit(solution)/shard_map/reduce_scatter | solution.py:41
  104.4 6.3 %collective-permute-start.3 = (bf16[96,768]{1,0:T(8,128)(2,1)S(1)}, bf16[96,768]{1,0:T(8,128)(2,1)S(1)}, u32[]{:S(2)}, u32[]{:S(2)}) collective-permute-start(bf16[96,768]{1,0:T(8,128)(2,1)S(1)} %pad_maximum_fusion.12), channel_id=1, source_target_pairs={{0,30},{1,31},{2,0},{3,1},{4,2},{5,3},{6,4},{7,5},{8,6},{9,7},{10,... | collective-permute-start | bytes 442376 | tf_op jit(solution)/shard_map/ppermute | solution.py:54
  110.8 8.4 %collective-permute-start.4 = (bf16[192,768]{1,0:T(8,128)(2,1)S(1)}, bf16[192,768]{1,0:T(8,128)(2,1)S(1)}, u32[]{:S(2)}, u32[]{:S(2)}) collective-permute-start(bf16[192,768]{1,0:T(8,128)(2,1)S(1)} %pad_maximum_fusion.11), channel_id=1, source_target_pairs={{0,28},{1,29},{2,30},{3,31},{4,0},{5,1},{6,2},{7,3},{8,4},{9,5},{1... | collective-permute-start | bytes 884744 | tf_op jit(solution)/shard_map/ppermute | solution.py:54
  119.2 13.8 %collective-permute-start.5 = (bf16[384,768]{1,0:T(8,128)(2,1)S(1)}, bf16[384,768]{1,0:T(8,128)(2,1)S(1)}, u32[]{:S(2)}, u32[]{:S(2)}) collective-permute-start(bf16[384,768]{1,0:T(8,128)(2,1)S(1)} %pad_maximum_fusion.2), channel_id=1, source_target_pairs={{0,24},{1,25},{2,26},{3,27},{4,28},{5,29},{6,30},{7,31},{8,0},{9,1... | collective-permute-start | bytes 1769480 | tf_op jit(solution)/shard_map/ppermute | solution.py:54
  133.0 1.2 copy-start.4
  134.2 70.1 %collective-permute-start.6 = (bf16[768,768]{1,0:T(8,128)(2,1)}, bf16[768,768]{1,0:T(8,128)(2,1)S(1)}, u32[]{:S(2)}, u32[]{:S(2)}) collective-permute-start(bf16[768,768]{1,0:T(8,128)(2,1)} %get-tuple-element.26), channel_id=1, source_target_pairs={{0,16},{1,17},{2,18},{3,19},{4,20},{5,21},{6,22},{7,23},{8,24},{9,... | collective-permute-start | bytes 3538952 | tf_op jit(solution)/shard_map/ppermute | solution.py:54
  204.3 3.8 copy-start.5
  208.1 2.0 copy-start.2
  213.3 0.9 copy-start.8
  214.2 0.9 copy-start.10
  222.2 1.5 copy-start
  222.3 9.2 %collective-permute-start.8 = (bf16[2,32,768]{2,1,0:T(8,128)(2,1)S(1)}, bf16[2,32,768]{2,1,0:T(8,128)(2,1)S(1)}, u32[]{:S(2)}, u32[]{:S(2)}) collective-permute-start(bf16[2,32,768]{2,1,0:T(8,128)(2,1)S(1)} %get-tuple-element.29), channel_id=1, source_target_pairs={{0,1},{1,2},{2,3},{3,4},{4,5},{5,6},{6,7},{7,8},{8,9},{9,10},{10,1... | collective-permute-start | bytes 294920 | tf_op jit(solution)/shard_map/ppermute | solution.py:17
  230.0 8.5 %copy-start.12 = (f32[1536]{0:T(1024)S(1)}, f32[1536]{0:T(1024)}, u32[]{:S(2)}) copy-start(f32[1536]{0:T(1024)} %param.10) | copy-start | bytes 18436
  230.0 8.5 %copy-start.14 = (f32[2,128]{1,0:T(2,128)S(1)}, f32[2,128]{1,0:T(2,128)}, u32[]{:S(2)}) copy-start(f32[2,128]{1,0:T(2,128)} %copy-done.13) | copy-start | bytes 3076
  230.0 8.4 %collective-permute-start.7 = (bf16[2,32,768]{2,1,0:T(8,128)(2,1)S(1)}, bf16[2,32,768]{2,1,0:T(8,128)(2,1)S(1)}, u32[]{:S(2)}, u32[]{:S(2)}) collective-permute-start(bf16[2,32,768]{2,1,0:T(8,128)(2,1)S(1)} %get-tuple-element.28), channel_id=1, source_target_pairs={{1,0},{2,1},{3,2},{4,3},{5,4},{6,5},{7,6},{8,7},{9,8},{10,9},{11,1... | collective-permute-start | bytes 294920 | tf_op jit(solution)/shard_map/ppermute | solution.py:20
  234.0 53.6 %copy-start.3 = (bf16[2,128,1536]{2,1,0:T(8,128)(2,1)S(1)}, bf16[2,128,1536]{2,1,0:T(8,128)(2,1)}, u32[]{:S(2)}) copy-start(bf16[2,128,1536]{2,1,0:T(8,128)(2,1)} %param.7) | copy-start | bytes 2359300
Sparse Core Ops, SparseCore 0:
  10.9 75.5 all-gather.1
  103.6 122.0 reduce-scatter.6
  233.3 161.9 reduce-scatter.4
